TPU v7x, 256 devices: a whole 4x4x8 slice. The times are simulated.
256 devices in a mesh: lat: 8 (over x_hi, y), lon: 32 (over x_lo, z, core).
Axes of the slice: x: 4 (x_hi: 2, x_lo: 2; x = x_hi * 2 + x_lo), y: 4, z: 8, core: 2. Of those that a mesh axis runs over, the one named last changes fastest.
Arguments:
- sea_state: bfloat16 [64, 256, 4096], P(None, 'lat', 'lon'), may hold values from -60 to 60
- conv_kernel: bfloat16 [64, 49], replicated, may hold values from -0.875 to 0.875
- conv_bias: bfloat16 [64], replicated, may hold values from -3 to 3
- norm_gain: bfloat16 [64], replicated, may hold values from 0.25 to 1.75
- norm_shift: bfloat16 [64], replicated, may hold values from -3 to 3
- w_in: bfloat16 [64, 256], replicated, may hold values from -0.75 to 0.75
- b_in: bfloat16 [256], replicated, may hold values from -3 to 3
- w_out: bfloat16 [256, 64], replicated, may hold values from -0.375 to 0.375
- b_out: bfloat16 [64], replicated, may hold values from -3 to 3
- layer_scale: bfloat16 [64], replicated, may hold values from 0.29882812 to 1
- sea_mask: int32 [256, 4096], P('lat', 'lon'), may hold values 0 or 1
- cotangent: bfloat16 [64, 256, 4096], P(None, 'lat', 'lon'), may hold values from -6 to 6
Outputs:
- new_state: bfloat16 [64, 256, 4096], P(None, 'lat', 'lon')
- state_grad: bfloat16 [64, 256, 4096], P(None, 'lat', 'lon')
- kernel_grad: float32 [64, 49], replicated
- w_in_grad: float32 [64, 256], replicated
- w_out_grad: float32 [256, 64], replicated
- b_in_grad: float32 [256], replicated
- channel_grads: float32 [5, 64], replicated
Inputs may be any that keep to these rules, and one draw needn't show every extreme that they name: `sea_mask`: 1 marks an ocean cell, 0 land.
All inputs are finite; a program needn't handle non-finite values. No bound on the sum of `sea_mask` on one device may be relied on, other than what follows from the above.
Results may differ from a plain program's by a relative error of at most 0.0062.
Values sent between devices are 32-bit elements; how exact they have to be, the bound alone decides.
No kernel may reach another device: no remote copies, remote signals or barrier semaphores. Data moves between devices by JAX's collectives and lax.ppermute only.
A program may use at most 128 MiB of HBM per device.

v0:
```python
import math
import jax
import jax.numpy as jnp
from jax import lax
from jax.sharding import PartitionSpec as P

slope_coef = 0.044715
tanh_scale = math.sqrt(2.0 / math.pi)
ln_epsilon = 1e-06


def with_halo(value, sides, width, wrap):
    for axis, dim in sides:
        size, length = (lax.axis_size(axis), value.shape[dim])
        up = [(i, (i + 1) % size) for i in range(size if wrap else size - 1)]
        down = [(j, i) for i, j in up]
        last = lax.slice_in_dim(value, length - width, length, axis=dim)
        initial = lax.slice_in_dim(value, 0, width, axis=dim)
        before = lax.ppermute(last, axis, up)
        after = lax.ppermute(initial, axis, down)
        value = jnp.concatenate([before, value, after], axis=dim)
    return value


def depthwise(padded, conv_kernel, conv_bias, row_count, col_count):
    weights = conv_kernel.astype(jnp.float32)
    running = (
        jnp.zeros((padded.shape[0], row_count, col_count), jnp.float32)
        + conv_bias.astype(jnp.float32)[:, None, None]
    )
    for row_off in range(7):
        for col_off in range(7):
            window = padded[:, row_off : row_off + row_count, col_off : col_off + col_count]
            running = running + weights[:, 7 * row_off + col_off][:, None, None] * window
    return running


def kernel_grads(padded, conv_grad):
    row_count = conv_grad.shape[1]
    col_count = conv_grad.shape[2]
    columns = []
    for row_off in range(7):
        for col_off in range(7):
            window = padded[:, row_off : row_off + row_count, col_off : col_off + col_count]
            columns.append(jnp.sum(conv_grad * window, axis=(1, 2)))
    return jnp.stack(columns, axis=1)


def spread_back(conv_grad, conv_kernel):
    row_count = conv_grad.shape[1]
    col_count = conv_grad.shape[2]
    weights = conv_kernel.astype(jnp.float32)
    widened = jnp.pad(conv_grad, ((0, 0), (6, 6), (6, 6)))
    running = jnp.zeros((conv_grad.shape[0], row_count + 6, col_count + 6), jnp.float32)
    for row_off in range(7):
        for col_off in range(7):
            window = widened[
                :, 6 - row_off : 12 - row_off + row_count, 6 - col_off : 12 - col_off + col_count
            ]
            running = running + weights[:, 7 * row_off + col_off][:, None, None] * window
    return running


def pointwise(
    conv_out,
    sea_state,
    cotangent,
    sea_mask,
    norm_gain,
    norm_shift,
    w_in,
    b_in,
    w_out,
    b_out,
    layer_scale,
):
    chan_count = conv_out.shape[0]
    flat_conv = conv_out.reshape(chan_count, -1)
    centre = flat_conv - jnp.mean(flat_conv, axis=0, keepdims=True)
    inv_std = lax.rsqrt(jnp.mean(centre * centre, axis=0, keepdims=True) + ln_epsilon)
    unit_norm = centre * inv_std
    gain_col = norm_gain.astype(jnp.float32)[:, None]
    normed = (unit_norm * gain_col + norm_shift.astype(jnp.float32)[:, None]).astype(jnp.bfloat16)
    pre_act = (
        jnp.dot(w_in.T, normed, preferred_element_type=jnp.float32)
        + b_in.astype(jnp.float32)[:, None]
    )
    tangent = jnp.tanh(tanh_scale * (pre_act + slope_coef * pre_act * pre_act * pre_act))
    hidden = (0.5 * pre_act * (1.0 + tangent)).astype(jnp.bfloat16)
    mixed_out = (
        jnp.dot(w_out.T, hidden, preferred_element_type=jnp.float32)
        + b_out.astype(jnp.float32)[:, None]
    )
    ocean_mask = sea_mask.reshape(1, -1).astype(jnp.float32)
    scale_col = layer_scale.astype(jnp.float32)[:, None]
    state_flat = sea_state.reshape(chan_count, -1).astype(jnp.float32)
    new_state = (ocean_mask * (state_flat + scale_col * mixed_out)).astype(jnp.bfloat16)
    masked_cot = ocean_mask * cotangent.reshape(chan_count, -1).astype(jnp.float32)
    mixed_grad = (scale_col * masked_cot).astype(jnp.bfloat16)
    scale_sum = jnp.sum(masked_cot * mixed_out, axis=1)
    out_bias_sum = jnp.sum(mixed_grad.astype(jnp.float32), axis=1)
    cell_axes = (((1,), (1,)), ((), ()))
    out_weight_sum = lax.dot_general(
        hidden, mixed_grad, cell_axes, preferred_element_type=jnp.float32
    )
    hidden_grad = jnp.dot(w_out, mixed_grad, preferred_element_type=jnp.float32)
    gelu_slope = 0.5 * (1.0 + tangent) + 0.5 * pre_act * (1.0 - tangent * tangent) * tanh_scale * (
        1.0 + 3.0 * slope_coef * pre_act * pre_act
    )
    pre_grad = (hidden_grad * gelu_slope).astype(jnp.bfloat16)
    in_bias_sum = jnp.sum(pre_grad.astype(jnp.float32), axis=1)
    in_weight_sum = lax.dot_general(normed, pre_grad, cell_axes, preferred_element_type=jnp.float32)
    normed_grad = jnp.dot(w_in, pre_grad, preferred_element_type=jnp.float32)
    gain_sum = jnp.sum(normed_grad * unit_norm, axis=1)
    shift_sum = jnp.sum(normed_grad, axis=1)
    unit_grad = normed_grad * gain_col
    conv_grad = inv_std * (
        unit_grad
        - jnp.mean(unit_grad, axis=0, keepdims=True)
        - unit_norm * jnp.mean(unit_grad * unit_norm, axis=0, keepdims=True)
    )
    partial_sums = (
        scale_sum,
        out_bias_sum,
        out_weight_sum,
        in_bias_sum,
        in_weight_sum,
        gain_sum,
        shift_sum,
    )
    return (
        new_state.reshape(conv_out.shape),
        conv_grad.reshape(conv_out.shape),
        masked_cot.reshape(conv_out.shape),
        partial_sums,
    )


def lon_extend(values):
    return with_halo(values, (("lon", 2),), 3, True)


def lat_extend(values):
    return with_halo(values, (("lat", 1),), 3, False)


def fold_partner(top_rows):
    lon_count = lax.axis_size("lon")
    pieces = top_rows.reshape(lon_count, -1)
    scattered = lax.all_to_all(pieces, "lon", split_axis=0, concat_axis=0, tiled=True)
    collected = lax.all_to_all(scattered[::-1], "lon", split_axis=0, concat_axis=0, tiled=True)
    return collected.reshape(top_rows.shape)


def fold_columns(values, col_count):
    col_rims = jnp.concatenate([values[:, :, :3], values[:, :, col_count + 3 :]], axis=2)
    col_from = lon_extend(col_rims)
    folded = values[:, :, 3 : col_count + 3]
    folded = folded.at[:, :, :3].add(col_from[:, :, :3])
    return folded.at[:, :, col_count - 3 :].add(col_from[:, :, 9:])


def fold_rows(values, row_count, on_top):
    row_rims = jnp.concatenate([values[:, :3], values[:, row_count + 3 :]], axis=1)
    row_from = lat_extend(row_rims)
    folded = values[:, 3 : row_count + 3]
    folded = folded.at[:, :3].add(row_from[:, :3])
    folded = folded.at[:, row_count - 3 :].add(row_from[:, 9:])
    returned = fold_partner(values[:, row_count + 3 :])[:, ::-1, ::-1]
    return folded.at[:, row_count - 3 :].add(jnp.where(on_top, returned, 0.0))


def per_device(
    sea_state,
    conv_kernel,
    conv_bias,
    norm_gain,
    norm_shift,
    w_in,
    b_in,
    w_out,
    b_out,
    layer_scale,
    sea_mask,
    cotangent,
):
    chan_count, row_count, col_count = sea_state.shape
    on_top = lax.axis_index("lat") == lax.axis_size("lat") - 1
    widened = sea_state.astype(jnp.float32)
    tall_field = lat_extend(widened)
    mirrored = fold_partner(widened[:, row_count - 3 :, :])[:, ::-1, ::-1]
    tall_field = jnp.concatenate(
        [
            tall_field[:, : row_count + 3],
            jnp.where(on_top, mirrored, tall_field[:, row_count + 3 :]),
        ],
        axis=1,
    )
    padded = lon_extend(tall_field)
    conv_out = depthwise(padded, conv_kernel, conv_bias, row_count, col_count)
    new_state, conv_grad, masked_cot, partial_sums = pointwise(
        conv_out,
        sea_state,
        cotangent,
        sea_mask,
        norm_gain,
        norm_shift,
        w_in,
        b_in,
        w_out,
        b_out,
        layer_scale,
    )
    scale_sum, out_bias_sum, out_weight_sum, in_bias_sum, in_weight_sum, gain_sum, shift_sum = (
        partial_sums
    )
    kernel_sum = kernel_grads(padded, conv_grad)
    bias_sum = jnp.sum(conv_grad, axis=(1, 2))
    spread = spread_back(conv_grad, conv_kernel)
    grid_grad = fold_rows(fold_columns(spread, col_count), row_count, on_top)
    state_grad = (masked_cot + grid_grad).astype(jnp.bfloat16)
    totals = lax.psum(
        (
            kernel_sum,
            bias_sum,
            gain_sum,
            shift_sum,
            out_bias_sum,
            scale_sum,
            in_weight_sum,
            out_weight_sum,
            in_bias_sum,
        ),
        ("lat", "lon"),
    )
    (
        kernel_total,
        bias_total,
        gain_total,
        shift_total,
        out_bias_total,
        scale_total,
        in_weight_total,
        out_weight_total,
        in_bias_total,
    ) = totals
    grad_scale = 1.0 / math.sqrt(
        row_count * lax.axis_size("lat") * col_count * lax.axis_size("lon")
    )
    channel_grads = grad_scale * jnp.stack(
        [bias_total, gain_total, shift_total, out_bias_total, scale_total]
    )
    return (
        new_state,
        state_grad,
        grad_scale * kernel_total,
        grad_scale * in_weight_total,
        grad_scale * out_weight_total,
        grad_scale * in_bias_total,
        channel_grads,
    )


def solution(mesh):
    placed = (
        P(None, "lat", "lon"),
        P(),
        P(),
        P(),
        P(),
        P(),
        P(),
        P(),
        P(),
        P(),
        P("lat", "lon"),
        P(None, "lat", "lon"),
    )
    return jax.shard_map(
        per_device,
        mesh=mesh,
        in_specs=placed,
        out_specs=(P(None, "lat", "lon"), P(None, "lat", "lon"), P(), P(), P(), P(), P()),
        check_vma=False,
    )
```

profile of v0, /device:TPU:1, one launch (start us, length us, event | category | flops | bytes accessed | tf_op | source)
XLA Modules:
  0.0 568.7 jit_solution(2259703244371274148)
XLA Ops:
  8.3 4.0 collective-permute-start
  13.1 10.5 %all-to-all-start = ((f32[32,1,768]{2,1,0:T(1,128)}), f32[32,1,768]{2,1,0:T(1,128)S(1)}, u32[]{:S(2)}, u32[]{:S(2)}) async-start(f32[32,1,768]{2,1,0:T(1,128)} %all_to_all.38), calls=%async_computation | async-start | bytes 196608 | tf_op jit(solution)/shard_map/all_to_all | solution.py:150
  29.2 2.8 all-to-all-done
  32.8 5.6 all-to-all-start.1
  39.3 7.5 %all-to-all-done.1 = f32[32,1,768]{2,1,0:T(1,128)S(1)} async-done(((f32[32,1,768]{2,1,0:T(1,128)}), f32[32,1,768]{2,1,0:T(1,128)S(1)}, u32[]{:S(2)}, u32[]{:S(2)}) %all-to-all-start.1) | async-done | bytes 98336 | tf_op jit(solution)/shard_map/all_to_all | solution.py:151
  59.4 5.1 maximum_maximum_fusion
  64.6 37.4 %fusion.121 = (f32[32,128]{1,0:T(8,128)S(1)}, f32[64,32,128]{2,1,0:T(8,128)}) fusion(f32[64,38,131]{2,1,0:T(8,128)} %get-tuple-element.148, f32[64]{0:T(128)S(1)} %get-tuple-element.158, f32[64]{0:T(128)S(1)} %get-tuple-element.159, f32[64]{0:T(128)S(1)} %get-tuple-element.160, f32[64,3,128]{2,1,0:T(4,128)S(1)} %broadcast_select_fusion, ...), kind=kLoop, calls=%fused_computation.319 | loop fusion | flops 27521024 | bytes 46363136 | tf_op jit(solution)/shard_map/reduce_sum | solution.py:79
  103.4 4.7 multiply_convert_fusion
  108.1 4.5 convert_reduce_fusion
  115.7 8.1 %multiply_reduce_fusion.5 = (f32[64]{0:T(128)}, f32[64]{0:T(128)}, f32[64]{0:T(128)}, f32[64]{0:T(128)}, f32[64]{0:T(128)}, /*index=5*/f32[64]{0:T(128)}, f32[64...) fusion(f32[64,38,131]{2,1,0:T(8,128)S(1)} %get-tuple-element.14, ...), kind=kLoop, calls=%fused_computation.195 | loop fusion | flops 9436032 | bytes 19927552 | tf_op jit(solution)/shard_map/reduce_sum | solution.py:45
  124.2 28.6 %multiply_reduce_fusion.1 = (f32[64]{0:T(128)}, f32[64]{0:T(128)}, f32[64]{0:T(128)}, f32[64]{0:T(128)}, f32[64]{0:T(128)}, /*index=5*/f32[64]{0:T(128)}, f32[64...) fusion(f32[64,38,131]{2,1,0:T(8,128)} %get-tuple-element.148, ...), kind=kLoop, calls=%fused_computation.191 | loop fusion | flops 9436032 | bytes 19927552 | tf_op jit(solution)/shard_map/reduce_sum | solution.py:45
  154.3 35.2 %fusion.104 = f32[64,38,134]{2,1,0:T(8,128)S(1)} fusion(f32[64,32,128]{2,1,0:T(8,128)S(1)} %bitcast.300, f32[64]{0:T(128)S(1)} %get-tuple-element.158, f32[64]{0:T(128)S(1)} %copy-done.14, f32[64]{0:T(128)S(1)} %copy-done.16, f32[64]{0:T(128)S(1)} %copy-done.18, f32[64]{0:T(128)S(1)} %copy-done.20, f32[64]{0:T(128)S(1)} %copy-done.22, f32[64]{0:T(128)S(1)} %copy-done.24, ...), kind=kLoop, calls=%fused_computation.160 | loop fusion | flops 31611136 | bytes 2364672 | tf_op jit(solution)/shard_map/add | solution.py:60
  189.5 2.7 fusion.122
  207.2 3.4 fusion.117
  210.6 4.4 multiply_reduce_fusion
  216.3 9.0 %multiply_reduce_fusion.4 = (f32[64]{0:T(128)S(1)}, f32[64]{0:T(128)S(1)}, f32[64]{0:T(128)S(1)}, f32[64]{0:T(128)S(1)}, f32[64]{0:T(128)S(1)}, /*index=5*/f32[6...) fusion(f32[64,3,128]{2,1,0:T(4,128)S(1)} %broadcast_select_fusi, ...), kind=kLoop, calls=%fused_computation.194 | loop fusion | flops 7863552 | bytes 8588288 | tf_op jit(solution)/shard_map/reduce_sum | solution.py:45
  227.2 7.1 %scatter-add.16 = f32[64,38,128]{2,1,0:T(8,128)} dynamic-update-slice(f32[64,38,128]{2,1,0:T(8,128)} %slice.995, f32[64,38,3]{2,1,0:T(8,128)S(1)} %copy.27, s32[]{:T(128)} %constant.160.clone.1, s32[]{:T(128)} %constant.160.clone.1, s32[]{:T(128)} %constant.160.clone.1) | dynamic-update-slice | bytes 58372 | tf_op jit(solution)/shard_map/scatter-add | solution.py:159
  238.0 21.4 %scatter-add.19 = f32[64,38,128]{2,1,0:T(8,128)S(1)} dynamic-update-slice(f32[64,38,128]{2,1,0:T(8,128)S(1)} %copy-done.5, f32[64,38,3]{2,1,0:T(8,128)S(1)} %copy.30, s32[]{:T(128)} %constant.160.clone.1, s32[]{:T(128)} %constant.160.clone.1, s32[]{:T(128)} %constant.161.clone.1) | dynamic-update-slice | bytes 58372 | tf_op jit(solution)/shard_map/scatter-add | solution.py:160
  259.7 4.3 collective-permute-start.6
  264.7 7.6 %all-to-all-start.2 = ((f32[32,1,768]{2,1,0:T(1,128)}), f32[32,1,768]{2,1,0:T(1,128)S(1)}, u32[]{:S(2)}, u32[]{:S(2)}) async-start(f32[32,1,768]{2,1,0:T(1,128)} %all_to_all.39), calls=%async_computation.2 | async-start | bytes 196608 | tf_op jit(solution)/shard_map/all_to_all | solution.py:150
  273.7 188.9 %all-reduce.5.cloned.1.call-done = (f32[64,256]{1,0:T(8,128)}, f32[256,64]{0,1:T(8,128)}) async-done(((f32[64,256]{1,0:T(8,128)}, f32[256,64]{0,1:T(8,128)}), (f32[64,256]{1,0:T(8,128)}, f32[256,64]{0,1:T(8,128)})) %all-reduce.5.cloned.1.call-update) | async-done | bytes 131088 | tf_op jit(solution)/shard_map/psum | solution.py:222
  466.5 6.6 %all-to-all-start.3 = ((f32[32,1,768]{2,1,0:T(1,128)}), f32[32,1,768]{2,1,0:T(1,128)S(1)}, u32[]{:S(2)}, u32[]{:S(2)}) async-start(f32[32,1,768]{2,1,0:T(1,128)} %copy.32), calls=%async_computation.3 | async-start | bytes 196608 | tf_op jit(solution)/shard_map/all_to_all | solution.py:151
  473.6 7.9 %all-to-all-done.3 = f32[32,1,768]{2,1,0:T(1,128)S(1)} async-done(((f32[32,1,768]{2,1,0:T(1,128)}), f32[32,1,768]{2,1,0:T(1,128)S(1)}, u32[]{:S(2)}, u32[]{:S(2)}) %all-to-all-start.3) | async-done | bytes 98336 | tf_op jit(solution)/shard_map/all_to_all | solution.py:151
  485.4 74.4 %all-reduce.1 = (f32[64,49]{0,1:T(8,128)S(1)}, f32[256]{0:T(256)S(1)}, f32[1,64]{1,0:T(1,128)S(1)}, f32[1,64]{1,0:T(1,128)S(1)}, f32[1,64]{1,0:T(1,128)S(1)}, /*index=5*/f32[1,64]{1,0:T(1,128)S(1)}, f32[1,64]{1,0:T(1,128)S(1)}) all-reduce(f32[64,49]{0,1:T(8,128)S(1)} %stack.217, ...), channel_id=1, replica_groups=mesh['lat'=8,'lon'=32] {'lat','lon'}, use_global_device_ids=true, to_apply=%region_53.54 | all-reduce | flops 3712 | bytes 29696 | tf_op jit(solution)/shard_map/psum | solution.py:222
  (318 shorter events, 60.9 us)
Async XLA Ops:
  7.2 96.2 %copy-start = (bf16[64,256]{1,0:T(8,128)(2,1)S(1)}, bf16[64,256]{1,0:T(8,128)(2,1)}, u32[]{:S(2)}) copy-start(bf16[64,256]{1,0:T(8,128)(2,1)} %param.27) | copy-start | bytes 98308
  8.3 39.1 %collective-permute-start = (f32[64,3,128]{2,1,0:T(4,128)S(1)}, f32[64,3,128]{2,1,0:T(4,128)S(1)}, u32[]{:S(2)}, u32[]{:S(2)}) collective-permute-start(f32[64,3,128]{2,1,0:T(4,128)S(1)} %get-tuple-element.156), channel_id=1, source_target_pairs={{0,32},{32,64},{64,96},{96,128},{128,160},{160,192},{192,224},{1,3... | collective-permute-start | bytes 294920 | tf_op jit(solution)/shard_map/ppermute | solution.py:19
  13.1 18.9 %all-to-all-start = ((f32[32,1,768]{2,1,0:T(1,128)}), f32[32,1,768]{2,1,0:T(1,128)S(1)}, u32[]{:S(2)}, u32[]{:S(2)}) async-start(f32[32,1,768]{2,1,0:T(1,128)} %all_to_all.38), calls=%async_computation | async-start | bytes 196608 | tf_op jit(solution)/shard_map/all_to_all | solution.py:150
  23.6 23.8 %collective-permute-start.1 = (f32[64,3,128]{2,1,0:T(4,128)S(1)}, f32[64,3,128]{2,1,0:T(4,128)S(1)}, u32[]{:S(2)}, u32[]{:S(2)}) collective-permute-start(f32[64,3,128]{2,1,0:T(4,128)S(1)} %get-tuple-element.155), channel_id=1, source_target_pairs={{32,0},{64,32},{96,64},{128,96},{160,128},{192,160},{224,192},{33,... | collective-permute-start | bytes 294920 | tf_op jit(solution)/shard_map/ppermute | solution.py:20
  29.1 35.4 %copy-start.13 = (f32[64]{0:T(128)}, f32[64]{0:T(128)S(1)}, u32[]{:S(2)}) copy-start(f32[64]{0:T(128)S(1)} %get-tuple-element.159) | copy-start | bytes 772
  29.1 35.4 %copy-start.15 = (f32[64]{0:T(128)}, f32[64]{0:T(128)S(1)}, u32[]{:S(2)}) copy-start(f32[64]{0:T(128)S(1)} %get-tuple-element.160) | copy-start | bytes 772
  29.1 35.4 %copy-start.17 = (f32[64]{0:T(128)}, f32[64]{0:T(128)S(1)}, u32[]{:S(2)}) copy-start(f32[64]{0:T(128)S(1)} %get-tuple-element.161) | copy-start | bytes 772
  29.1 35.4 %copy-start.19 = (f32[64]{0:T(128)}, f32[64]{0:T(128)S(1)}, u32[]{:S(2)}) copy-start(f32[64]{0:T(128)S(1)} %get-tuple-element.162) | copy-start | bytes 772
  29.1 35.4 %copy-start.21 = (f32[64]{0:T(128)}, f32[64]{0:T(128)S(1)}, u32[]{:S(2)}) copy-start(f32[64]{0:T(128)S(1)} %get-tuple-element.163) | copy-start | bytes 772
  29.1 35.4 %copy-start.23 = (f32[64]{0:T(128)}, f32[64]{0:T(128)S(1)}, u32[]{:S(2)}) copy-start(f32[64]{0:T(128)S(1)} %get-tuple-element.164) | copy-start | bytes 772
  29.1 35.4 %copy-start.25 = (f32[64]{0:T(128)}, f32[64]{0:T(128)S(1)}, u32[]{:S(2)}) copy-start(f32[64]{0:T(128)S(1)} %get-tuple-element.165) | copy-start | bytes 772
  29.1 35.4 %copy-start.27 = (f32[64]{0:T(128)}, f32[64]{0:T(128)S(1)}, u32[]{:S(2)}) copy-start(f32[64]{0:T(128)S(1)} %get-tuple-element.166) | copy-start | bytes 772
  32.8 13.9 %all-to-all-start.1 = ((f32[32,1,768]{2,1,0:T(1,128)}), f32[32,1,768]{2,1,0:T(1,128)S(1)}, u32[]{:S(2)}, u32[]{:S(2)}) async-start(f32[32,1,768]{2,1,0:T(1,128)} %copy.20), calls=%async_computation.1 | async-start | bytes 196608 | tf_op jit(solution)/shard_map/all_to_all | solution.py:151
  38.4 424.2 %all-reduce.5.cloned.1.call-start = ((), (), s32[]{:S(2)}) async-start(), calls=%async_computation.4 | async-start | bytes 262144 | tf_op jit(solution)/shard_map/psum | solution.py:222
  50.9 5.2 collective-permute-start.2
  53.3 4.4 collective-permute-start.3
  115.7 38.2 %copy-start.2 = (f32[8,8,32,128]{3,2,1,0:T(8,128)}, f32[8,8,32,128]{3,2,1,0:T(8,128)S(1)}, u32[]{:S(2)}) copy-start(f32[8,8,32,128]{3,2,1,0:T(8,128)S(1)} %copy.39) | copy-start | bytes 3145732
  197.6 28.2 %collective-permute-start.4 = (f32[64,38,3]{0,1,2:T(8,128)}, f32[64,38,3]{0,1,2:T(8,128)}, u32[]{:S(2)}, u32[]{:S(2)}) collective-permute-start(f32[64,38,3]{0,1,2:T(8,128)} %copy.25), channel_id=1, source_target_pairs={{0,1},{1,2},{2,3},{3,4},{4,5},{5,6},{6,7},{7,8},{8,9},{9,10},{10,1... | collective-permute-start | bytes 87560 | tf_op jit(solution)/shard_map/ppermute | solution.py:19
  203.5 33.1 %collective-permute-start.5 = (f32[64,38,3]{0,1,2:T(8,128)}, f32[64,38,3]{0,1,2:T(8,128)}, u32[]{:S(2)}, u32[]{:S(2)}) collective-permute-start(f32[64,38,3]{0,1,2:T(8,128)} %copy.28), channel_id=1, source_target_pairs={{1,0},{2,1},{3,2},{4,3},{5,4},{6,5},{7,6},{8,7},{9,8},{10,9},{11,1... | collective-permute-start | bytes 87560 | tf_op jit(solution)/shard_map/ppermute | solution.py:20
  259.5 224.3 %copy-start.11 = (bf16[64,32,128]{2,1,0:T(8,128)(2,1)S(1)}, bf16[64,32,128]{2,1,0:T(8,128)(2,1)}, u32[]{:S(2)}) copy-start(bf16[64,32,128]{2,1,0:T(8,128)(2,1)} %param.33) | copy-start | bytes 1572868
  259.7 213.4 %collective-permute-start.6 = (f32[64,3,128]{2,1,0:T(4,128)S(1)}, f32[64,3,128]{2,1,0:T(4,128)S(1)}, u32[]{:S(2)}, u32[]{:S(2)}) collective-permute-start(f32[64,3,128]{2,1,0:T(4,128)S(1)} %get-tuple-element.146), channel_id=1, source_target_pairs={{0,32},{32,64},{64,96},{96,128},{128,160},{160,192},{192,224},{1,3... | collective-permute-start | bytes 294920 | tf_op jit(solution)/shard_map/ppermute | solution.py:19
  264.7 200.8 %all-to-all-start.2 = ((f32[32,1,768]{2,1,0:T(1,128)}), f32[32,1,768]{2,1,0:T(1,128)S(1)}, u32[]{:S(2)}, u32[]{:S(2)}) async-start(f32[32,1,768]{2,1,0:T(1,128)} %all_to_all.39), calls=%async_computation.2 | async-start | bytes 196608 | tf_op jit(solution)/shard_map/all_to_all | solution.py:150
  272.4 209.7 %collective-permute-start.7 = (f32[64,3,128]{2,1,0:T(4,128)S(1)}, f32[64,3,128]{2,1,0:T(4,128)}, u32[]{:S(2)}, u32[]{:S(2)}) collective-permute-start(f32[64,3,128]{2,1,0:T(4,128)S(1)} %get-tuple-element.145), channel_id=1, source_target_pairs={{32,0},{64,32},{96,64},{128,96},{160,128},{192,160},{224,192},{33,... | collective-permute-start | bytes 294920 | tf_op jit(solution)/shard_map/ppermute | solution.py:20
  466.5 15.0 %all-to-all-start.3 = ((f32[32,1,768]{2,1,0:T(1,128)}), f32[32,1,768]{2,1,0:T(1,128)S(1)}, u32[]{:S(2)}, u32[]{:S(2)}) async-start(f32[32,1,768]{2,1,0:T(1,128)} %copy.32), calls=%async_computation.3 | async-start | bytes 196608 | tf_op jit(solution)/shard_map/all_to_all | solution.py:151
  (104 other events, 1818.0 us)
Sparse Core Ops, SparseCore 0:
  216.0 246.5 all-reduce.4
where the time goes:
time: 576 us; the launch traced here: 569 us
  waiting for transfers between devices  207 us (36%)
  other arithmetic  145 us (25%)
  blocking collectives  74.4 us (13%)
  local copies, waits for them, and re-layouts  59.6 us (10%)
  starting transfers between devices  46.8 us (8%)
  matrix products  19.5 us (3%)
  between operations  16.1 us (3%)
    psum x1, waiting for transfers between devices, per_device(): lax.psum((kernel_sum, bias_sum, gain_sum, shift_sum, out_bias_sum, scale_...  189 us
    psum x1, blocking collectives, per_device(): lax.psum((kernel_sum, bias_sum, gain_sum, shift_sum, out_bias_sum, scale_...  74.4 us
    reduce_sum x4, other arithmetic, kernel_grads(): columns.append(jnp.sum(conv_grad * window, axis=(1, 2)))  46.8 us
    reduce_sum x1, other arithmetic, pointwise(): centre = flat_conv - jnp.mean(flat_conv, axis=0, keepdims=True)  37.4 us
    add x1, other arithmetic, spread_back(): running + weights[:, 7 * row_off + col_off][:, None, None] * window  35.2 us
    scatter-add x1, local copies, waits for them, and re-layouts, fold_columns(): return folded.at[:, :, col_count - 3:].add(col_from[:, :, 9:])  21.4 us
    all_to_all x2, starting transfers between devices, fold_partner(): lax.all_to_all(pieces, 'lon', split_axis=0, concat_axis=0, tiled=True)  18.1 us
    all_to_all x2, waiting for transfers between devices, fold_partner(): lax.all_to_all(scattered[::-1], 'lon', split_axis=0, concat_axis=0, tiled...  15.3 us
  transfers between devices with their start and end apart: 13, of which 4 were waited for; matrix products, arithmetic and copies ran while one was open for 13% of the time, Pallas kernels for 0%

commit v1 on v0

--- a/solution.py
+++ b/solution.py
@@ -219,20 +219,19 @@
     spread = spread_back(conv_grad, conv_kernel)
     grid_grad = fold_rows(fold_columns(spread, col_count), row_count, on_top)
     state_grad = (masked_cot + grid_grad).astype(jnp.bfloat16)
-    totals = lax.psum(
-        (
-            kernel_sum,
-            bias_sum,
-            gain_sum,
-            shift_sum,
-            out_bias_sum,
-            scale_sum,
-            in_weight_sum,
-            out_weight_sum,
-            in_bias_sum,
-        ),
-        ("lat", "lon"),
-    )
+    totals = (
+        kernel_sum,
+        bias_sum,
+        gain_sum,
+        shift_sum,
+        out_bias_sum,
+        scale_sum,
+        in_weight_sum,
+        out_weight_sum,
+        in_bias_sum,
+    )
+    for mesh_axis in ("lat", "lon"):
+        totals = lax.psum(totals, mesh_axis)
     (
         kernel_total,
         bias_total,

time: 576 us -> 675 us (1.17)
  blocking collectives: 74.4 us -> 142 us
  waiting for transfers between devices: 207 us -> 223 us
  starting transfers between devices: 46.8 us -> 54.4 us
    psum x1 -> x2, blocking collectives: 74.4 us -> 142 us  [per_device(): totals = lax.psum(totals, mesh_axis)]
    psum x1 -> x2, waiting for transfers between devices: 189 us -> 212 us  [per_device(): totals = lax.psum(totals, mesh_axis)]
    all_to_all x2, waiting for transfers between devices: 15.3 us -> 7.49 us  [fold_partner(): lax.all_to_all(scattered[::-1], 'lon', split_axis=0, concat_axis=0, tiled...]
  transfers between devices with their start and end apart: 13 -> 14, of which waited for: 4 -> 4; matrix products, arithmetic and copies ran while one was open for 13% -> 12% of each run, Pallas kernels for 0% -> 0%
where the time goes in v1:
time: 675 us; the launch traced here: 666 us
  waiting for transfers between devices  223 us (33%)
  other arithmetic  144 us (21%)
  blocking collectives  142 us (21%)
  local copies, waits for them, and re-layouts  65.5 us (10%)
  starting transfers between devices  54.4 us (8%)
  matrix products  21.4 us (3%)
  between operations  15.9 us (2%)
    psum x2, waiting for transfers between devices, per_device(): totals = lax.psum(totals, mesh_axis)  212 us
    psum x2, blocking collectives, per_device(): totals = lax.psum(totals, mesh_axis)  142 us
    reduce_sum x4, other arithmetic, kernel_grads(): columns.append(jnp.sum(conv_grad * window, axis=(1, 2)))  46.4 us
    reduce_sum x1, other arithmetic, pointwise(): centre = flat_conv - jnp.mean(flat_conv, axis=0, keepdims=True)  37.3 us
    add x1, other arithmetic, spread_back(): running + weights[:, 7 * row_off + col_off][:, None, None] * window  34.6 us
    all_to_all x2, starting transfers between devices, fold_partner(): lax.all_to_all(scattered[::-1], 'lon', split_axis=0, concat_axis=0, tiled...  18.9 us
    all_to_all x2, starting transfers between devices, fold_partner(): lax.all_to_all(pieces, 'lon', split_axis=0, concat_axis=0, tiled=True)  18.1 us
    scatter-add x1, local copies, waits for them, and re-layouts, fold_columns(): return folded.at[:, :, col_count - 3:].add(col_from[:, :, 9:])  18 us
  transfers between devices with their start and end apart: 14, of which 4 were waited for; matrix products, arithmetic and copies ran while one was open for 12% of the time, Pallas kernels for 0%

profile of v1, /device:TPU:1, one launch (start us, length us, event | category | flops | bytes accessed | tf_op | source)
XLA Modules:
  0.0 665.7 jit_solution(13306825924163939246)
XLA Ops:
  8.3 4.0 collective-permute-start
  13.1 10.5 %all-to-all-start = ((f32[32,1,768]{2,1,0:T(1,128)}), f32[32,1,768]{2,1,0:T(1,128)S(1)}, u32[]{:S(2)}, u32[]{:S(2)}) async-start(f32[32,1,768]{2,1,0:T(1,128)} %all_to_all.38), calls=%async_computation | async-start | bytes 196608 | tf_op jit(solution)/shard_map/all_to_all | solution.py:150
  32.8 5.4 all-to-all-start.1
  39.1 7.5 %all-to-all-done.1 = f32[32,1,768]{2,1,0:T(1,128)S(1)} async-done(((f32[32,1,768]{2,1,0:T(1,128)}), f32[32,1,768]{2,1,0:T(1,128)S(1)}, u32[]{:S(2)}, u32[]{:S(2)}) %all-to-all-start.1) | async-done | bytes 98336 | tf_op jit(solution)/shard_map/all_to_all | solution.py:151
  59.1 5.1 maximum_maximum_fusion
  64.2 37.3 %fusion.121 = (f32[32,128]{1,0:T(8,128)S(1)}, f32[64,32,128]{2,1,0:T(8,128)}) fusion(f32[64,38,131]{2,1,0:T(8,128)} %get-tuple-element.157, f32[64]{0:T(128)S(1)} %get-tuple-element.167, f32[64]{0:T(128)S(1)} %get-tuple-element.168, f32[64]{0:T(128)S(1)} %get-tuple-element.169, f32[64,3,128]{2,1,0:T(4,128)S(1)} %broadcast_select_fusion, ...), kind=kLoop, calls=%fused_computation.319 | loop fusion | flops 27521024 | bytes 46363136 | tf_op jit(solution)/shard_map/reduce_sum | solution.py:79
  103.0 4.7 multiply_convert_fusion
  107.7 4.5 convert_reduce_fusion
  115.3 8.1 %multiply_reduce_fusion.5 = (f32[64]{0:T(128)}, f32[64]{0:T(128)}, f32[64]{0:T(128)}, f32[64]{0:T(128)}, f32[64]{0:T(128)}, /*index=5*/f32[64]{0:T(128)}, f32[64...) fusion(f32[64,38,131]{2,1,0:T(8,128)S(1)} %get-tuple-element.15, ...), kind=kLoop, calls=%fused_computation.195 | loop fusion | flops 9436032 | bytes 19927552 | tf_op jit(solution)/shard_map/reduce_sum | solution.py:45
  123.3 28.6 %multiply_reduce_fusion.1 = (f32[64]{0:T(128)}, f32[64]{0:T(128)}, f32[64]{0:T(128)}, f32[64]{0:T(128)}, f32[64]{0:T(128)}, /*index=5*/f32[64]{0:T(128)}, f32[64...) fusion(f32[64,38,131]{2,1,0:T(8,128)} %get-tuple-element.157, ...), kind=kLoop, calls=%fused_computation.191 | loop fusion | flops 9436032 | bytes 19927552 | tf_op jit(solution)/shard_map/reduce_sum | solution.py:45
  152.3 3.4 fusion.120
  156.0 34.6 %fusion.104 = f32[64,38,134]{2,1,0:T(8,128)S(1)} fusion(f32[64,32,128]{2,1,0:T(8,128)S(1)} %bitcast.300, f32[64]{0:T(128)S(1)} %get-tuple-element.167, f32[64]{0:T(128)S(1)} %get-tuple-element.168, f32[64]{0:T(128)S(1)} %get-tuple-element.169, f32[64]{0:T(128)S(1)} %get-tuple-element.170, f32[64]{0:T(128)S(1)} %get-tuple-element.171, ...), kind=kLoop, calls=%fused_computation.160 | loop fusion | flops 31611136 | bytes 2364672 | tf_op jit(solution)/shard_map/add | solution.py:60
  203.8 3.4 fusion.117
  207.1 4.4 multiply_reduce_fusion
  212.4 9.1 %multiply_reduce_fusion.4 = (f32[64]{0:T(128)}, f32[64]{0:T(128)}, f32[64]{0:T(128)}, f32[64]{0:T(128)}, f32[64]{0:T(128)}, /*index=5*/f32[64]{0:T(128)}, f32[64...) fusion(f32[64,3,128]{2,1,0:T(4,128)S(1)} %broadcast_select_fusion, ...), kind=kLoop, calls=%fused_computation.194 | loop fusion | flops 7863552 | bytes 8588288 | tf_op jit(solution)/shard_map/reduce_sum | solution.py:45
  226.1 11.2 %scatter-add.16 = f32[64,38,128]{2,1,0:T(8,128)S(1)} dynamic-update-slice(f32[64,38,128]{2,1,0:T(8,128)S(1)} %slice.995, f32[64,38,3]{2,1,0:T(8,128)} %copy.27, s32[]{:T(128)} %constant.160.clone.1, s32[]{:T(128)} %constant.160.clone.1, s32[]{:T(128)} %constant.160.clone.1) | dynamic-update-slice | bytes 58372 | tf_op jit(solution)/shard_map/scatter-add | solution.py:159
  242.5 18.0 %scatter-add.19 = f32[64,38,128]{2,1,0:T(8,128)S(1)} dynamic-update-slice(f32[64,38,128]{2,1,0:T(8,128)S(1)} %scatter-add.16, f32[64,38,3]{2,1,0:T(8,128)} %copy.30, s32[]{:T(128)} %constant.160.clone.1, s32[]{:T(128)} %constant.160.clone.1, s32[]{:T(128)} %constant.161.clone.1) | dynamic-update-slice | bytes 58372 | tf_op jit(solution)/shard_map/scatter-add | solution.py:160
  261.2 5.1 collective-permute-start.6
  271.1 7.6 %all-to-all-start.2 = ((f32[32,1,768]{2,1,0:T(1,128)}), f32[32,1,768]{2,1,0:T(1,128)S(1)}, u32[]{:S(2)}, u32[]{:S(2)}) async-start(f32[32,1,768]{2,1,0:T(1,128)} %all_to_all.39), calls=%async_computation.2 | async-start | bytes 196608 | tf_op jit(solution)/shard_map/all_to_all | solution.py:150
  280.0 18.1 %all-reduce.10.cloned.1.call-done = (f32[64,256]{1,0:T(8,128)}, f32[256,64]{0,1:T(8,128)}) async-done(((f32[64,256]{1,0:T(8,128)}, f32[256,64]{0,1:T(8,128)}), (f32[64,256]{1,0:T(8,128)}, f32[256,64]{0,1:T(8,128)})) %all-reduce.10.cloned.1.call-update) | async-done | bytes 131088 | tf_op jit(solution)/shard_map/psum | solution.py:234
  300.5 13.5 %all-to-all-start.3 = ((f32[32,1,768]{2,1,0:T(1,128)}), f32[32,1,768]{2,1,0:T(1,128)S(1)}, u32[]{:S(2)}, u32[]{:S(2)}) async-start(f32[32,1,768]{2,1,0:T(1,128)} %copy.32), calls=%async_computation.3 | async-start | bytes 196608 | tf_op jit(solution)/shard_map/all_to_all | solution.py:151
  314.0 194.1 %all-reduce.8.cloned.1.call-done = (f32[64,256]{1,0:T(8,128)}, f32[256,64]{0,1:T(8,128)}) async-done(((f32[64,256]{1,0:T(8,128)}, f32[256,64]{0,1:T(8,128)}), (f32[64,256]{1,0:T(8,128)}, f32[256,64]{0,1:T(8,128)})) %all-reduce.8.cloned.1.call-update) | async-done | bytes 131088 | tf_op jit(solution)/shard_map/psum | solution.py:234
  515.0 34.2 %all-reduce.3 = (f32[64,49]{0,1:T(8,128)S(1)}, f32[256]{0:T(256)S(1)}, f32[64]{0:T(128)S(1)}, f32[64]{0:T(128)S(1)}, f32[64]{0:T(128)S(1)}, /*index=5*/f32[64]{0:T(128)S(1)}, f32[64]{0:T(128)S(1)}) all-reduce(f32[64,49]{0,1:T(8,128)S(1)} %stack.217, f32[256]{0:T(256)S(1)} %copy-done.91, ...), channel_id=1, replica_groups=mesh['lat'=8,'lon'=32] {'lat'}, use_global_device_ids=true, to_apply=%region_53.54 | all-reduce | flops 3712 | bytes 29696 | tf_op jit(solution)/shard_map/psum | solution.py:234
  549.2 107.6 %all-reduce.1 = (f32[64,49]{0,1:T(8,128)S(1)}, f32[256]{0:T(256)S(1)}, f32[1,64]{1,0:T(1,128)S(1)}, f32[1,64]{1,0:T(1,128)S(1)}, f32[1,64]{1,0:T(1,128)S(1)}, /*index=5*/f32[1,64]{1,0:T(1,128)S(1)}, f32[1,64]{1,0:T(1,128)S(1)}) all-reduce(f32[64,49]{0,1:T(8,128)S(1)} %get-tuple-element.137, ...), channel_id=1, replica_groups=mesh['lat'=8,'lon'=32] {'lon'}, use_global_device_ids=true, to_apply=%region_54.55 | all-reduce | flops 3712 | bytes 29696 | tf_op jit(solution)/shard_map/psum | solution.py:234
  (292 shorter events, 69.8 us)
Async XLA Ops:
  7.2 95.8 %copy-start = (bf16[64,256]{1,0:T(8,128)(2,1)S(1)}, bf16[64,256]{1,0:T(8,128)(2,1)}, u32[]{:S(2)}) copy-start(bf16[64,256]{1,0:T(8,128)(2,1)} %param.27) | copy-start | bytes 98308
  7.2 31.7 %copy-start.10 = (bf16[64,32,128]{2,1,0:T(8,128)(2,1)S(1)}, bf16[64,32,128]{2,1,0:T(8,128)(2,1)}, u32[]{:S(2)}) copy-start(bf16[64,32,128]{2,1,0:T(8,128)(2,1)} %param.22) | copy-start | bytes 1572868
  8.3 38.9 %collective-permute-start = (f32[64,3,128]{2,1,0:T(4,128)S(1)}, f32[64,3,128]{2,1,0:T(4,128)S(1)}, u32[]{:S(2)}, u32[]{:S(2)}) collective-permute-start(f32[64,3,128]{2,1,0:T(4,128)S(1)} %get-tuple-element.165), channel_id=1, source_target_pairs={{0,32},{32,64},{64,96},{96,128},{128,160},{160,192},{192,224},{1,3... | collective-permute-start | bytes 294920 | tf_op jit(solution)/shard_map/ppermute | solution.py:19
  13.1 18.9 %all-to-all-start = ((f32[32,1,768]{2,1,0:T(1,128)}), f32[32,1,768]{2,1,0:T(1,128)S(1)}, u32[]{:S(2)}, u32[]{:S(2)}) async-start(f32[32,1,768]{2,1,0:T(1,128)} %all_to_all.38), calls=%async_computation | async-start | bytes 196608 | tf_op jit(solution)/shard_map/all_to_all | solution.py:150
  23.6 23.6 %collective-permute-start.1 = (f32[64,3,128]{2,1,0:T(4,128)S(1)}, f32[64,3,128]{2,1,0:T(4,128)S(1)}, u32[]{:S(2)}, u32[]{:S(2)}) collective-permute-start(f32[64,3,128]{2,1,0:T(4,128)S(1)} %get-tuple-element.164), channel_id=1, source_target_pairs={{32,0},{64,32},{96,64},{128,96},{160,128},{192,160},{224,192},{33,... | collective-permute-start | bytes 294920 | tf_op jit(solution)/shard_map/ppermute | solution.py:20
  32.8 13.7 %all-to-all-start.1 = ((f32[32,1,768]{2,1,0:T(1,128)}), f32[32,1,768]{2,1,0:T(1,128)S(1)}, u32[]{:S(2)}, u32[]{:S(2)}) async-start(f32[32,1,768]{2,1,0:T(1,128)} %copy.20), calls=%async_computation.1 | async-start | bytes 196608 | tf_op jit(solution)/shard_map/all_to_all | solution.py:151
  38.2 259.9 %all-reduce.10.cloned.1.call-start = ((), (), s32[]{:S(2)}) async-start(), calls=%async_computation.5 | async-start | bytes 262144 | tf_op jit(solution)/shard_map/psum | solution.py:234
  50.8 5.2 collective-permute-start.2
  53.2 4.4 collective-permute-start.3
  115.3 40.5 %copy-start.2 = (f32[8,8,32,128]{3,2,1,0:T(8,128)}, f32[8,8,32,128]{3,2,1,0:T(8,128)S(1)}, u32[]{:S(2)}) copy-start(f32[8,8,32,128]{3,2,1,0:T(8,128)S(1)} %copy.39) | copy-start | bytes 3145732
  123.3 28.6 %copy-start.93 = (f32[64]{0:T(128)S(1)}, f32[64]{0:T(128)}, u32[]{:S(2)}) copy-start(f32[64]{0:T(128)} %convert_element_type.92) | copy-start | bytes 772
  195.9 27.8 %collective-permute-start.4 = (f32[64,38,3]{0,1,2:T(8,128)}, f32[64,38,3]{0,1,2:T(8,128)}, u32[]{:S(2)}, u32[]{:S(2)}) collective-permute-start(f32[64,38,3]{0,1,2:T(8,128)} %copy.25), channel_id=1, source_target_pairs={{0,1},{1,2},{2,3},{3,4},{4,5},{5,6},{6,7},{7,8},{8,9},{9,10},{10,1... | collective-permute-start | bytes 87560 | tf_op jit(solution)/shard_map/ppermute | solution.py:19
  200.0 40.5 %collective-permute-start.5 = (f32[64,38,3]{0,1,2:T(8,128)}, f32[64,38,3]{0,1,2:T(8,128)S(1)}, u32[]{:S(2)}, u32[]{:S(2)}) collective-permute-start(f32[64,38,3]{0,1,2:T(8,128)} %copy.28), channel_id=1, source_target_pairs={{1,0},{2,1},{3,2},{4,3},{5,4},{6,5},{7,6},{8,7},{9,8},{10,9},{11,1... | collective-permute-start | bytes 87560 | tf_op jit(solution)/shard_map/ppermute | solution.py:20
  261.2 36.9 %collective-permute-start.6 = (f32[64,3,128]{2,1,0:T(4,128)S(1)}, f32[64,3,128]{2,1,0:T(4,128)}, u32[]{:S(2)}, u32[]{:S(2)}) collective-permute-start(f32[64,3,128]{2,1,0:T(4,128)S(1)} %get-tuple-element.155), channel_id=1, source_target_pairs={{0,32},{32,64},{64,96},{96,128},{128,160},{160,192},{192,224},{1,3... | collective-permute-start | bytes 294920 | tf_op jit(solution)/shard_map/ppermute | solution.py:19
  270.1 243.2 %copy-start.11 = (bf16[64,32,128]{2,1,0:T(8,128)(2,1)S(1)}, bf16[64,32,128]{2,1,0:T(8,128)(2,1)}, u32[]{:S(2)}) copy-start(bf16[64,32,128]{2,1,0:T(8,128)(2,1)} %param.33) | copy-start | bytes 1572868
  271.1 28.6 %all-to-all-start.2 = ((f32[32,1,768]{2,1,0:T(1,128)}), f32[32,1,768]{2,1,0:T(1,128)S(1)}, u32[]{:S(2)}, u32[]{:S(2)}) async-start(f32[32,1,768]{2,1,0:T(1,128)} %all_to_all.39), calls=%async_computation.2 | async-start | bytes 196608 | tf_op jit(solution)/shard_map/all_to_all | solution.py:150
  278.7 229.4 %all-reduce.8.cloned.1.call-start = ((), (), s32[]{:S(2)}) async-start(), calls=%async_computation.4 | async-start | bytes 262144 | tf_op jit(solution)/shard_map/psum | solution.py:234
  278.7 232.9 %collective-permute-start.7 = (f32[64,3,128]{2,1,0:T(4,128)S(1)}, f32[64,3,128]{2,1,0:T(4,128)}, u32[]{:S(2)}, u32[]{:S(2)}) collective-permute-start(f32[64,3,128]{2,1,0:T(4,128)S(1)} %copy-done.12), channel_id=1, source_target_pairs={{32,0},{64,32},{96,64},{128,96},{160,128},{192,160},{224,192},{33,... | collective-permute-start | bytes 294920 | tf_op jit(solution)/shard_map/ppermute | solution.py:20
  299.1 215.8 %copy-start.85 = (f32[64]{0:T(128)S(1)}, f32[64]{0:T(128)}, u32[]{:S(2)}) copy-start(f32[64]{0:T(128)} %reduce_sum.587) | copy-start | bytes 772
  299.1 215.8 %copy-start.86 = (f32[64]{0:T(128)S(1)}, f32[64]{0:T(128)}, u32[]{:S(2)}) copy-start(f32[64]{0:T(128)} %get-tuple-element.115) | copy-start | bytes 772
  299.2 215.8 %copy-start.87 = (f32[64]{0:T(128)S(1)}, f32[64]{0:T(128)}, u32[]{:S(2)}) copy-start(f32[64]{0:T(128)} %get-tuple-element.116) | copy-start | bytes 772
  299.2 215.8 %copy-start.88 = (f32[64]{0:T(128)S(1)}, f32[64]{0:T(128)}, u32[]{:S(2)}) copy-start(f32[64]{0:T(128)} %get-tuple-element.160) | copy-start | bytes 772
  299.2 215.8 %copy-start.91 = (f32[256]{0:T(256)S(1)}, f32[256]{0:T(256)}, u32[]{:S(2)}) copy-start(f32[256]{0:T(256)} %get-tuple-element.222) | copy-start | bytes 3076
  300.5 210.5 %all-to-all-start.3 = ((f32[32,1,768]{2,1,0:T(1,128)}), f32[32,1,768]{2,1,0:T(1,128)S(1)}, u32[]{:S(2)}, u32[]{:S(2)}) async-start(f32[32,1,768]{2,1,0:T(1,128)} %copy.32), calls=%async_computation.3 | async-start | bytes 196608 | tf_op jit(solution)/shard_map/all_to_all | solution.py:151
  (90 other events, 1196.3 us)
Sparse Core Ops, SparseCore 0:
  212.6 85.5 all-reduce.9
  300.8 207.2 all-reduce.7
